TPU v7x, 32 devices: a whole 2x2x4 slice. The times are simulated.
32 devices in a mesh: win: 2 (over y), gz: 4 (over z), gy: 2 (over x), gx: 2 (over core).
Axes of the slice: x: 2, y: 2, z: 4, core: 2. Of those that a mesh axis runs over, the one named last changes fastest.
Arguments:
- noisy: float32 [32, 16, 256], P(('win', 'gz'), 'gy', 'gx'), parts along dimension 0, may hold values from -6 to 6
- first_weight: float32 [32, 1, 27], replicated, may hold values from -1.25 to 1.25
- first_bias: float32 [16], replicated, may hold values from -8 to -3
- second_weight: float32 [32, 16, 27], replicated, may hold values from -0.3125 to 0.3125
- second_bias: float32 [16], replicated, may hold values from -8 to -3
- head_weight: float32 [16], replicated, may hold values from -18 to 18
- seg_weight_in: float32 [16, 1, 27], replicated, may hold values from -1.25 to 1.25
- seg_bias_in: float32 [16], replicated, may hold values from -3 to 3
- seg_weight_out: float32 [16, 16, 27], replicated, may hold values from -0.3125 to 0.3125
- seg_bias_out: float32 [16], replicated, may hold values from -3 to 3
Outputs:
- denoised: float32 [32, 16, 256], P(('win', 'gz'), 'gy', 'gx'), parts along dimension 0
- segmented: float32 [16, 32, 16, 256], P(None, ('win', 'gz'), 'gy', 'gx'), parts along dimension 1
There are 2 independent parts, one for each index of `win`. A program takes and returns all parts, laid end to end along the dimension named above; an argument that names none is the same for every part. Nothing has to cross between parts.
All inputs are finite; a program needn't handle non-finite values.
Results may differ from a plain program's by a relative error of at most 0.00029.
Values sent between devices are 32-bit elements; how exact they have to be, the bound alone decides.
A program may use at most 64 MiB of HBM per device.

v0:
```python
import jax
import jax.numpy as jnp
from jax import lax
from jax.sharding import PartitionSpec as P


def shifted(value, axis, steps):
    count = lax.axis_size(axis)
    first, last = (max(0, -steps), min(count, count - steps))
    return lax.ppermute(value, axis, [(source, source + steps) for source in range(first, last)])


def with_halo(block, sides, width):
    for axis, dim in sides:
        count = lax.axis_size(axis)
        forward = [(i, i + 1) for i in range(count - 1)]
        backward = [(target, source) for source, target in forward]
        low = lax.ppermute(
            lax.slice_in_dim(block, block.shape[dim] - width, None, axis=dim), axis, forward
        )
        high = lax.ppermute(lax.slice_in_dim(block, 0, width, axis=dim), axis, backward)
        block = jnp.concatenate([low, block, high], axis=dim)
    return block


def convolve(padded, weight):
    depth = padded.shape[1] - 2
    height = padded.shape[2] - 2
    width = padded.shape[3] - 2
    total = jnp.zeros((weight.shape[0], depth, height, width), jnp.float32)
    for tap in range(27):
        step_z = tap // 9
        step_y = tap // 3 % 3
        step_x = tap % 3
        piece = padded[
            :, step_z : step_z + depth, step_y : step_y + height, step_x : step_x + width
        ]
        total = total + jnp.einsum(
            "oc,czyx->ozyx", weight[:, :, tap], piece, precision=lax.Precision.HIGHEST
        )
    return total


def affine(earlier, later):
    return (earlier[0] * later[0], later[0] * earlier[1] + later[1])


def recurrent(padded, weight, bias, backward):
    channels = bias.shape[0]
    pre = convolve(padded, weight)
    cand = jnp.tanh(pre[:channels])
    keep = jax.nn.sigmoid(-(pre[channels:] + bias[:, None, None, None]))
    inject = (1.0 - keep) * cand
    if backward:
        keep = jnp.flip(keep, 1)
        inject = jnp.flip(inject, 1)
    cum_keep, cum_inject = lax.associative_scan(affine, (keep, inject), axis=1)
    total_keep = cum_keep[:, -1]
    total_inject = cum_inject[:, -1]
    offset = -1 if backward else 1

    def relay(turn, carry):
        return shifted(total_keep * carry + total_inject, "gz", offset)

    carry = lax.fori_loop(0, lax.axis_size("gz") - 1, relay, jnp.zeros_like(total_inject))
    hidden = cum_keep * carry[:, None] + cum_inject
    if backward:
        hidden = jnp.flip(hidden, 1)
    return hidden


def inside_mask(length, where, count):
    places = jnp.arange(length + 2)
    outside = (places == 0) & (where == 0) | (places == length + 1) & (where == count - 1)
    return jnp.where(outside, 0.0, 1.0).astype(jnp.float32)


def body(
    noisy,
    first_weight,
    first_bias,
    second_weight,
    second_bias,
    head_weight,
    seg_weight_in,
    seg_bias_in,
    seg_weight_out,
    seg_bias_out,
):
    noisy_pad = with_halo(noisy[None], (("gz", 1), ("gy", 2), ("gx", 3)), 1)
    first_hidden = recurrent(noisy_pad, first_weight, first_bias, False)
    hidden_pad = with_halo(first_hidden, (("gz", 1), ("gy", 2), ("gx", 3)), 1)
    second_hidden = recurrent(hidden_pad, second_weight, second_bias, True)
    denoised = noisy + jnp.einsum(
        "c,czyx->zyx", head_weight, second_hidden, precision=lax.Precision.HIGHEST
    )
    deep_pad = with_halo(denoised[None], (("gz", 1), ("gy", 2), ("gx", 3)), 2)
    grown = jnp.maximum(convolve(deep_pad, seg_weight_in) + seg_bias_in[:, None, None, None], 0.0)
    mask_z = inside_mask(denoised.shape[0], lax.axis_index("gz"), lax.axis_size("gz"))
    mask_y = inside_mask(denoised.shape[1], lax.axis_index("gy"), lax.axis_size("gy"))
    mask_x = inside_mask(denoised.shape[2], lax.axis_index("gx"), lax.axis_size("gx"))
    feature_pad = (
        grown * (mask_z[:, None, None] * mask_y[None, :, None] * mask_x[None, None, :])[None]
    )
    segmented = convolve(feature_pad, seg_weight_out) + seg_bias_out[:, None, None, None]
    return (denoised, segmented)


def solution(mesh):
    in_specs = (P(("win", "gz"), "gy", "gx"), P(), P(), P(), P(), P(), P(), P(), P(), P())
    out_specs = (P(("win", "gz"), "gy", "gx"), P(None, ("win", "gz"), "gy", "gx"))
    return jax.shard_map(body, mesh=mesh, in_specs=in_specs, out_specs=out_specs, check_vma=False)
```

profile of v0, /device:TPU:0, one launch (start us, length us, event | category | flops | bytes accessed | tf_op | source)
XLA Modules:
  0.0 146.8 jit_solution(1202628407863394762)
XLA Ops:
  1.4 4.9 %collective-permute-start.2 = (f32[1,1,8,128]{3,2,1,0:T(8,128)S(1)}, f32[1,1,8,128]{3,2,1,0:T(8,128)S(1)}, u32[]{:S(2)}, u32[]{:S(2)}) collective-permute-start(f32[1,1,8,128]{3,2,1,0:T(8,128)S(1)} %get-tuple-element.241), channel_id=1, source_target_pairs={{0,4},{4,8},{8,12},{1,5},{5,9},{9,13},{2,6},{6,10},{10,14},{3,7},{... | collective-permute-start | bytes 12296 | tf_op jit(solution)/shard_map/ppermute | solution.py:18
  7.6 2.8 %fusion.224 = (f32[16,16,1]{2,1,0:T(8,128)}, f32[16,16,1]{2,1,0:T(8,128)}, f32[16,16,1]{2,1,0:T(8,128)}, f32[16,16,1]{2,1,0:T(8,128)}, f32[16,16,1]{2,1,0:T(8,12...) fusion(f32[16,16,27]{2,1,0:T(8,128)} %param.22), kind=kLoop, calls=%fused_computation.456 | loop fusion | bytes 16384 | tf_op jit(solution)/shard_map/slice | solution.py:39
  12.8 3.4 %collective-permute-start.4 = (f32[1,6,1,128]{3,2,1,0:T(1,128)S(1)}, f32[1,6,1,128]{3,2,1,0:T(1,128)S(1)}, u32[]{:S(2)}, u32[]{:S(2)}) collective-permute-start(f32[1,6,1,128]{3,2,1,0:T(1,128)S(1)} %get-tuple-element.235), channel_id=1, source_target_pairs={{0,2},{1,3},{4,6},{5,7},{8,10},{9,11},{12,14},{13,15},{16,18},{17,... | collective-permute-start | bytes 9224 | tf_op jit(solution)/shard_map/ppermute | solution.py:18
  17.5 4.2 %collective-permute-done.5 = f32[1,6,1,128]{3,2,1,0:T(1,128)S(1)} collective-permute-done((f32[1,6,1,128]{3,2,1,0:T(1,128)S(1)}, f32[1,6,1,128]{3,2,1,0:T(1,128)S(1)}, u32[]{:S(2)}, u32[]{:S(2)}) %collective-permute-start.5) | collective-permute-done | bytes 3104 | tf_op jit(solution)/shard_map/ppermute | solution.py:21
  24.4 1.8 %collective-permute-done.7 = f32[1,6,10,1]{3,2,1,0:T(8,128)S(1)} collective-permute-done((f32[1,6,10,1]{3,2,1,0:T(8,128)S(1)}, f32[1,6,10,1]{3,2,1,0:T(8,128)S(1)}, u32[]{:S(2)}, u32[]{:S(2)}) %collective-permute-start.7) | collective-permute-done | bytes 272 | tf_op jit(solution)/shard_map/ppermute | solution.py:21
  28.6 18.8 %while.20 = (s32[]{:T(128)}, f32[16,8,128]{2,1,0:T(8,128)S(1)}, f32[16,8,128]{2,1,0:T(8,128)S(1)}, f32[16,8,128]{2,1,0:T(8,128)S(1)}, s32[]{:T(128)}) while((s32[]{:T(128)}, f32[16,8,128]{2,1,0:T(8,128)S(1)}, f32[16,8,128]{2,1,0:T(8,128)S(1)}, f32[16,8,128]{2,1,0:T(8,128)S(1)}, s32[]{:T(128)}) %tuple.203), condition=%wide.region_1.0_spmd, body=%wide.region_0.0_spmd.sunk | while | flops 32770 | bytes 524389 | solution.py:65
  28.6 4.5 %collective-permute-start = (f32[16,8,128]{2,1,0:T(8,128)S(1)}, f32[16,8,128]{2,1,0:T(8,128)S(1)}, u32[]{:S(2)}, u32[]{:S(2)}) collective-permute-start(f32[16,8,128]{2,1,0:T(8,128)S(1)} %multiply_add_fusion.6), channel_id=1, source_target_pairs={{0,4},{4,8},{8,12},{1,5},{5,9},{9,13},{2,6},{6,10},{10,14},{3,7},{... | collective-permute-start | bytes 196616 | tf_op jit(solution)/shard_map/while/body/eval_jaxpr/ppermute | solution.py:10
  33.2 1.9 %collective-permute-done = f32[16,8,128]{2,1,0:T(8,128)S(1)} collective-permute-done((f32[16,8,128]{2,1,0:T(8,128)S(1)}, f32[16,8,128]{2,1,0:T(8,128)S(1)}, u32[]{:S(2)}, u32[]{:S(2)}) %collective-permute-start) | collective-permute-done | bytes 65568 | tf_op jit(solution)/shard_map/while/body/eval_jaxpr/ppermute | solution.py:10
  35.1 4.3 %collective-permute-start = (f32[16,8,128]{2,1,0:T(8,128)S(1)}, f32[16,8,128]{2,1,0:T(8,128)S(1)}, u32[]{:S(2)}, u32[]{:S(2)}) collective-permute-start(f32[16,8,128]{2,1,0:T(8,128)S(1)} %multiply_add_fusion.6), channel_id=1, source_target_pairs={{0,4},{4,8},{8,12},{1,5},{5,9},{9,13},{2,6},{6,10},{10,14},{3,7},{... | collective-permute-start | bytes 196616 | tf_op jit(solution)/shard_map/while/body/eval_jaxpr/ppermute | solution.py:10
  39.4 1.9 %collective-permute-done = f32[16,8,128]{2,1,0:T(8,128)S(1)} collective-permute-done((f32[16,8,128]{2,1,0:T(8,128)S(1)}, f32[16,8,128]{2,1,0:T(8,128)S(1)}, u32[]{:S(2)}, u32[]{:S(2)}) %collective-permute-start) | collective-permute-done | bytes 65568 | tf_op jit(solution)/shard_map/while/body/eval_jaxpr/ppermute | solution.py:10
  41.3 4.3 %collective-permute-start = (f32[16,8,128]{2,1,0:T(8,128)S(1)}, f32[16,8,128]{2,1,0:T(8,128)S(1)}, u32[]{:S(2)}, u32[]{:S(2)}) collective-permute-start(f32[16,8,128]{2,1,0:T(8,128)S(1)} %multiply_add_fusion.6), channel_id=1, source_target_pairs={{0,4},{4,8},{8,12},{1,5},{5,9},{9,13},{2,6},{6,10},{10,14},{3,7},{... | collective-permute-start | bytes 196616 | tf_op jit(solution)/shard_map/while/body/eval_jaxpr/ppermute | solution.py:10
  45.6 1.9 %collective-permute-done = f32[16,8,128]{2,1,0:T(8,128)S(1)} collective-permute-done((f32[16,8,128]{2,1,0:T(8,128)S(1)}, f32[16,8,128]{2,1,0:T(8,128)S(1)}, u32[]{:S(2)}, u32[]{:S(2)}) %collective-permute-start) | collective-permute-done | bytes 65568 | tf_op jit(solution)/shard_map/while/body/eval_jaxpr/ppermute | solution.py:10
  47.6 4.4 %collective-permute-start.8 = (f32[16,1,8,128]{3,0,2,1:T(8,128)S(1)}, f32[16,1,8,128]{3,0,2,1:T(8,128)S(1)}, u32[]{:S(2)}, u32[]{:S(2)}) collective-permute-start(f32[16,1,8,128]{3,0,2,1:T(8,128)S(1)} %get-tuple-element.129), channel_id=1, source_target_pairs={{0,4},{4,8},{8,12},{1,5},{5,9},{9,13},{2,6},{6,10},{10,14},{3,7},{... | collective-permute-start | bytes 196616 | tf_op jit(solution)/shard_map/ppermute | solution.py:18
  53.9 4.2 %collective-permute-done.9 = f32[16,1,8,128]{3,0,2,1:T(8,128)S(1)} collective-permute-done((f32[16,1,8,128]{3,0,2,1:T(8,128)S(1)}, f32[16,1,8,128]{3,0,2,1:T(8,128)S(1)}, u32[]{:S(2)}, u32[]{:S(2)}) %collective-permute-start.9) | collective-permute-done | bytes 65568 | tf_op jit(solution)/shard_map/ppermute | solution.py:21
  58.1 1.7 %collective-permute-start.10 = (f32[16,6,1,128]{3,0,2,1:T(8,128)S(1)}, f32[16,6,1,128]{3,0,2,1:T(8,128)S(1)}, u32[]{:S(2)}, u32[]{:S(2)}) collective-permute-start(f32[16,6,1,128]{3,0,2,1:T(8,128)S(1)} %get-tuple-element.119), channel_id=1, source_target_pairs={{0,2},{1,3},{4,6},{5,7},{8,10},{9,11},{12,14},{13,15},{16,18},{17,... | collective-permute-start | bytes 147464 | tf_op jit(solution)/shard_map/ppermute | solution.py:18
  62.4 3.4 %collective-permute-done.11 = f32[16,6,1,128]{3,0,2,1:T(8,128)S(1)} collective-permute-done((f32[16,6,1,128]{3,0,2,1:T(8,128)S(1)}, f32[16,6,1,128]{3,0,2,1:T(8,128)S(1)}, u32[]{:S(2)}, u32[]{:S(2)}) %collective-permute-start.11) | collective-permute-done | bytes 49184 | tf_op jit(solution)/shard_map/ppermute | solution.py:21
  86.7 19.1 %while.21 = (s32[]{:T(128)}, f32[16,8,128]{2,1,0:T(8,128)S(1)}, f32[16,8,128]{2,1,0:T(8,128)S(1)}, f32[16,8,128]{2,1,0:T(8,128)S(1)}, s32[]{:T(128)}) while((s32[]{:T(128)}, f32[16,8,128]{2,1,0:T(8,128)S(1)}, f32[16,8,128]{2,1,0:T(8,128)S(1)}, f32[16,8,128]{2,1,0:T(8,128)S(1)}, s32[]{:T(128)}) %tuple.206), condition=%wide.region_3.4_spmd, body=%wide.region_2.3_spmd.sunk | while | flops 32770 | bytes 524389 | solution.py:65
  88.0 5.4 %collective-permute-done.1 = f32[16,8,128]{2,1,0:T(8,128)S(1)} collective-permute-done((f32[16,8,128]{2,1,0:T(8,128)S(1)}, f32[16,8,128]{2,1,0:T(8,128)S(1)}, u32[]{:S(2)}, u32[]{:S(2)}) %collective-permute-start.1) | collective-permute-done | bytes 65568 | tf_op jit(solution)/shard_map/while/body/eval_jaxpr/ppermute | solution.py:10
  94.7 4.9 %collective-permute-done.1 = f32[16,8,128]{2,1,0:T(8,128)S(1)} collective-permute-done((f32[16,8,128]{2,1,0:T(8,128)S(1)}, f32[16,8,128]{2,1,0:T(8,128)S(1)}, u32[]{:S(2)}, u32[]{:S(2)}) %collective-permute-start.1) | collective-permute-done | bytes 65568 | tf_op jit(solution)/shard_map/while/body/eval_jaxpr/ppermute | solution.py:10
  100.9 4.9 %collective-permute-done.1 = f32[16,8,128]{2,1,0:T(8,128)S(1)} collective-permute-done((f32[16,8,128]{2,1,0:T(8,128)S(1)}, f32[16,8,128]{2,1,0:T(8,128)S(1)}, u32[]{:S(2)}, u32[]{:S(2)}) %collective-permute-start.1) | collective-permute-done | bytes 65568 | tf_op jit(solution)/shard_map/while/body/eval_jaxpr/ppermute | solution.py:10
  106.2 3.5 %collective-permute-start.14 = (f32[1,2,8,128]{3,2,1,0:T(8,128)S(1)}, f32[1,2,8,128]{3,2,1,0:T(8,128)S(1)}, u32[]{:S(2)}, u32[]{:S(2)}) collective-permute-start(f32[1,2,8,128]{3,2,1,0:T(8,128)S(1)} %get-tuple-element.237), channel_id=1, source_target_pairs={{0,4},{4,8},{8,12},{1,5},{5,9},{9,13},{2,6},{6,10},{10,14},{3,7},{... | collective-permute-start | bytes 24584 | tf_op jit(solution)/shard_map/ppermute | solution.py:18
  112.1 3.3 %collective-permute-done.15 = f32[1,2,8,128]{3,2,1,0:T(8,128)S(1)} collective-permute-done((f32[1,2,8,128]{3,2,1,0:T(8,128)S(1)}, f32[1,2,8,128]{3,2,1,0:T(8,128)S(1)}, u32[]{:S(2)}, u32[]{:S(2)}) %collective-permute-start.15) | collective-permute-done | bytes 8224 | tf_op jit(solution)/shard_map/ppermute | solution.py:21
  115.4 1.6 %collective-permute-start.16 = (f32[1,8,2,128]{3,2,1,0:T(2,128)S(1)}, f32[1,8,2,128]{3,2,1,0:T(2,128)S(1)}, u32[]{:S(2)}, u32[]{:S(2)}) collective-permute-start(f32[1,8,2,128]{3,2,1,0:T(2,128)S(1)} %get-tuple-element.229), channel_id=1, source_target_pairs={{0,2},{1,3},{4,6},{5,7},{8,10},{9,11},{12,14},{13,15},{16,18},{17,... | collective-permute-start | bytes 24584 | tf_op jit(solution)/shard_map/ppermute | solution.py:18
  131.6 3.0 %fusion.39 = f32[16,6,10,130]{3,0,2,1:T(8,128)S(1)} fusion(f32[6,10,130]{2,1,0:T(8,128)S(1)} %broadcast_multiply_fusion, f32[16]{0:T(128)S(1)} %copy-done.22, f32[16]{0:T(128)S(1)} %get-tuple-element.93, f32[6,10,130]{2,1,0:T(8,128)S(1)} %get-tuple-element.183, f32[16]{0:T(128)S(1)} %get-tuple-element.94, f32[6,10,130]{2,1,0:T(8,128)S(1)} %get-tuple-element.174, ...), kind=kLoop, calls=%fused_computation.82 | loop fusion | flops 6988800 | bytes 1374592 | tf_op jit(solution)/shard_map/mul | solution.py:103
  (241 shorter events, 68.8 us)
Async XLA Ops:
  1.4 10.8 %collective-permute-start.2 = (f32[1,1,8,128]{3,2,1,0:T(8,128)S(1)}, f32[1,1,8,128]{3,2,1,0:T(8,128)S(1)}, u32[]{:S(2)}, u32[]{:S(2)}) collective-permute-start(f32[1,1,8,128]{3,2,1,0:T(8,128)S(1)} %get-tuple-element.241), channel_id=1, source_target_pairs={{0,4},{4,8},{8,12},{1,5},{5,9},{9,13},{2,6},{6,10},{10,14},{3,7},{... | collective-permute-start | bytes 12296 | tf_op jit(solution)/shard_map/ppermute | solution.py:18
  6.3 5.8 %collective-permute-start.3 = (f32[1,1,8,128]{3,2,1,0:T(8,128)S(1)}, f32[1,1,8,128]{3,2,1,0:T(8,128)S(1)}, u32[]{:S(2)}, u32[]{:S(2)}) collective-permute-start(f32[1,1,8,128]{3,2,1,0:T(8,128)S(1)} %get-tuple-element.242), channel_id=1, source_target_pairs={{4,0},{8,4},{12,8},{5,1},{9,5},{13,9},{6,2},{10,6},{14,10},{7,3},{... | collective-permute-start | bytes 12296 | tf_op jit(solution)/shard_map/ppermute | solution.py:21
  12.8 4.7 %collective-permute-start.4 = (f32[1,6,1,128]{3,2,1,0:T(1,128)S(1)}, f32[1,6,1,128]{3,2,1,0:T(1,128)S(1)}, u32[]{:S(2)}, u32[]{:S(2)}) collective-permute-start(f32[1,6,1,128]{3,2,1,0:T(1,128)S(1)} %get-tuple-element.235), channel_id=1, source_target_pairs={{0,2},{1,3},{4,6},{5,7},{8,10},{9,11},{12,14},{13,15},{16,18},{17,... | collective-permute-start | bytes 9224 | tf_op jit(solution)/shard_map/ppermute | solution.py:18
  16.2 5.5 %collective-permute-start.5 = (f32[1,6,1,128]{3,2,1,0:T(1,128)S(1)}, f32[1,6,1,128]{3,2,1,0:T(1,128)S(1)}, u32[]{:S(2)}, u32[]{:S(2)}) collective-permute-start(f32[1,6,1,128]{3,2,1,0:T(1,128)S(1)} %get-tuple-element.236), channel_id=1, source_target_pairs={{2,0},{3,1},{6,4},{7,5},{10,8},{11,9},{14,12},{15,13},{18,16},{19,... | collective-permute-start | bytes 9224 | tf_op jit(solution)/shard_map/ppermute | solution.py:21
  21.7 2.6 %collective-permute-start.6 = (f32[1,6,10,1]{3,2,1,0:T(8,128)S(1)}, f32[1,6,10,1]{3,2,1,0:T(8,128)S(1)}, u32[]{:S(2)}, u32[]{:S(2)}) collective-permute-start(f32[1,6,10,1]{3,2,1,0:T(8,128)S(1)} %get-tuple-element.227), channel_id=1, source_target_pairs={{0,1},{2,3},{4,5},{6,7},{8,9},{10,11},{12,13},{14,15},{16,17},{18,... | collective-permute-start | bytes 728 | tf_op jit(solution)/shard_map/ppermute | solution.py:18
  23.0 3.1 %collective-permute-start.7 = (f32[1,6,10,1]{3,2,1,0:T(8,128)S(1)}, f32[1,6,10,1]{3,2,1,0:T(8,128)S(1)}, u32[]{:S(2)}, u32[]{:S(2)}) collective-permute-start(f32[1,6,10,1]{3,2,1,0:T(8,128)S(1)} %get-tuple-element.228), channel_id=1, source_target_pairs={{1,0},{3,2},{5,4},{7,6},{9,8},{11,10},{13,12},{15,14},{17,16},{19,... | collective-permute-start | bytes 728 | tf_op jit(solution)/shard_map/ppermute | solution.py:21
  28.6 6.4 %collective-permute-start = (f32[16,8,128]{2,1,0:T(8,128)S(1)}, f32[16,8,128]{2,1,0:T(8,128)S(1)}, u32[]{:S(2)}, u32[]{:S(2)}) collective-permute-start(f32[16,8,128]{2,1,0:T(8,128)S(1)} %multiply_add_fusion.6), channel_id=1, source_target_pairs={{0,4},{4,8},{8,12},{1,5},{5,9},{9,13},{2,6},{6,10},{10,14},{3,7},{... | collective-permute-start | bytes 196616 | tf_op jit(solution)/shard_map/while/body/eval_jaxpr/ppermute | solution.py:10
  35.1 6.2 %collective-permute-start = (f32[16,8,128]{2,1,0:T(8,128)S(1)}, f32[16,8,128]{2,1,0:T(8,128)S(1)}, u32[]{:S(2)}, u32[]{:S(2)}) collective-permute-start(f32[16,8,128]{2,1,0:T(8,128)S(1)} %multiply_add_fusion.6), channel_id=1, source_target_pairs={{0,4},{4,8},{8,12},{1,5},{5,9},{9,13},{2,6},{6,10},{10,14},{3,7},{... | collective-permute-start | bytes 196616 | tf_op jit(solution)/shard_map/while/body/eval_jaxpr/ppermute | solution.py:10
  41.3 6.2 %collective-permute-start = (f32[16,8,128]{2,1,0:T(8,128)S(1)}, f32[16,8,128]{2,1,0:T(8,128)S(1)}, u32[]{:S(2)}, u32[]{:S(2)}) collective-permute-start(f32[16,8,128]{2,1,0:T(8,128)S(1)} %multiply_add_fusion.6), channel_id=1, source_target_pairs={{0,4},{4,8},{8,12},{1,5},{5,9},{9,13},{2,6},{6,10},{10,14},{3,7},{... | collective-permute-start | bytes 196616 | tf_op jit(solution)/shard_map/while/body/eval_jaxpr/ppermute | solution.py:10
  47.6 6.3 %collective-permute-start.8 = (f32[16,1,8,128]{3,0,2,1:T(8,128)S(1)}, f32[16,1,8,128]{3,0,2,1:T(8,128)S(1)}, u32[]{:S(2)}, u32[]{:S(2)}) collective-permute-start(f32[16,1,8,128]{3,0,2,1:T(8,128)S(1)} %get-tuple-element.129), channel_id=1, source_target_pairs={{0,4},{4,8},{8,12},{1,5},{5,9},{9,13},{2,6},{6,10},{10,14},{3,7},{... | collective-permute-start | bytes 196616 | tf_op jit(solution)/shard_map/ppermute | solution.py:18
  52.0 6.2 %collective-permute-start.9 = (f32[16,1,8,128]{3,0,2,1:T(8,128)S(1)}, f32[16,1,8,128]{3,0,2,1:T(8,128)S(1)}, u32[]{:S(2)}, u32[]{:S(2)}) collective-permute-start(f32[16,1,8,128]{3,0,2,1:T(8,128)S(1)} %get-tuple-element.130), channel_id=1, source_target_pairs={{4,0},{8,4},{12,8},{5,1},{9,5},{13,9},{6,2},{10,6},{14,10},{7,3},{... | collective-permute-start | bytes 196616 | tf_op jit(solution)/shard_map/ppermute | solution.py:21
  58.1 4.2 %collective-permute-start.10 = (f32[16,6,1,128]{3,0,2,1:T(8,128)S(1)}, f32[16,6,1,128]{3,0,2,1:T(8,128)S(1)}, u32[]{:S(2)}, u32[]{:S(2)}) collective-permute-start(f32[16,6,1,128]{3,0,2,1:T(8,128)S(1)} %get-tuple-element.119), channel_id=1, source_target_pairs={{0,2},{1,3},{4,6},{5,7},{8,10},{9,11},{12,14},{13,15},{16,18},{17,... | collective-permute-start | bytes 147464 | tf_op jit(solution)/shard_map/ppermute | solution.py:18
  59.8 6.0 %collective-permute-start.11 = (f32[16,6,1,128]{3,0,2,1:T(8,128)S(1)}, f32[16,6,1,128]{3,0,2,1:T(8,128)S(1)}, u32[]{:S(2)}, u32[]{:S(2)}) collective-permute-start(f32[16,6,1,128]{3,0,2,1:T(8,128)S(1)} %get-tuple-element.120), channel_id=1, source_target_pairs={{2,0},{3,1},{6,4},{7,5},{10,8},{11,9},{14,12},{15,13},{18,16},{19,... | collective-permute-start | bytes 147464 | tf_op jit(solution)/shard_map/ppermute | solution.py:21
  66.0 6.5 %collective-permute-start.12 = (f32[16,6,10,1]{3,0,2,1:T(8,128)S(1)}, f32[16,6,10,1]{3,0,2,1:T(8,128)S(1)}, u32[]{:S(2)}, u32[]{:S(2)}) collective-permute-start(f32[16,6,10,1]{3,0,2,1:T(8,128)S(1)} %get-tuple-element.117), channel_id=1, source_target_pairs={{0,1},{2,3},{4,5},{6,7},{8,9},{10,11},{12,13},{14,15},{16,17},{18,... | collective-permute-start | bytes 11528 | tf_op jit(solution)/shard_map/ppermute | solution.py:18
  67.4 5.2 %collective-permute-start.13 = (f32[16,6,10,1]{3,0,2,1:T(8,128)S(1)}, f32[16,6,10,1]{3,0,2,1:T(8,128)S(1)}, u32[]{:S(2)}, u32[]{:S(2)}) collective-permute-start(f32[16,6,10,1]{3,0,2,1:T(8,128)S(1)} %get-tuple-element.118), channel_id=1, source_target_pairs={{1,0},{3,2},{5,4},{7,6},{9,8},{11,10},{13,12},{15,14},{17,16},{19,... | collective-permute-start | bytes 11528 | tf_op jit(solution)/shard_map/ppermute | solution.py:21
  86.7 6.7 %collective-permute-start.1 = (f32[16,8,128]{2,1,0:T(8,128)S(1)}, f32[16,8,128]{2,1,0:T(8,128)S(1)}, u32[]{:S(2)}, u32[]{:S(2)}) collective-permute-start(f32[16,8,128]{2,1,0:T(8,128)S(1)} %multiply_add_fusion.7), channel_id=1, source_target_pairs={{4,0},{8,4},{12,8},{5,1},{9,5},{13,9},{6,2},{10,6},{14,10},{7,3},{... | collective-permute-start | bytes 196616 | tf_op jit(solution)/shard_map/while/body/eval_jaxpr/ppermute | solution.py:10
  93.4 6.2 %collective-permute-start.1 = (f32[16,8,128]{2,1,0:T(8,128)S(1)}, f32[16,8,128]{2,1,0:T(8,128)S(1)}, u32[]{:S(2)}, u32[]{:S(2)}) collective-permute-start(f32[16,8,128]{2,1,0:T(8,128)S(1)} %multiply_add_fusion.7), channel_id=1, source_target_pairs={{4,0},{8,4},{12,8},{5,1},{9,5},{13,9},{6,2},{10,6},{14,10},{7,3},{... | collective-permute-start | bytes 196616 | tf_op jit(solution)/shard_map/while/body/eval_jaxpr/ppermute | solution.py:10
  99.6 6.2 %collective-permute-start.1 = (f32[16,8,128]{2,1,0:T(8,128)S(1)}, f32[16,8,128]{2,1,0:T(8,128)S(1)}, u32[]{:S(2)}, u32[]{:S(2)}) collective-permute-start(f32[16,8,128]{2,1,0:T(8,128)S(1)} %multiply_add_fusion.7), channel_id=1, source_target_pairs={{4,0},{8,4},{12,8},{5,1},{9,5},{13,9},{6,2},{10,6},{14,10},{7,3},{... | collective-permute-start | bytes 196616 | tf_op jit(solution)/shard_map/while/body/eval_jaxpr/ppermute | solution.py:10
  106.2 5.9 %collective-permute-start.14 = (f32[1,2,8,128]{3,2,1,0:T(8,128)S(1)}, f32[1,2,8,128]{3,2,1,0:T(8,128)S(1)}, u32[]{:S(2)}, u32[]{:S(2)}) collective-permute-start(f32[1,2,8,128]{3,2,1,0:T(8,128)S(1)} %get-tuple-element.237), channel_id=1, source_target_pairs={{0,4},{4,8},{8,12},{1,5},{5,9},{9,13},{2,6},{6,10},{10,14},{3,7},{... | collective-permute-start | bytes 24584 | tf_op jit(solution)/shard_map/ppermute | solution.py:18
  109.7 5.7 %collective-permute-start.15 = (f32[1,2,8,128]{3,2,1,0:T(8,128)S(1)}, f32[1,2,8,128]{3,2,1,0:T(8,128)S(1)}, u32[]{:S(2)}, u32[]{:S(2)}) collective-permute-start(f32[1,2,8,128]{3,2,1,0:T(8,128)S(1)} %get-tuple-element.238), channel_id=1, source_target_pairs={{4,0},{8,4},{12,8},{5,1},{9,5},{13,9},{6,2},{10,6},{14,10},{7,3},{... | collective-permute-start | bytes 24584 | tf_op jit(solution)/shard_map/ppermute | solution.py:21
  115.4 10.2 %collective-permute-start.16 = (f32[1,8,2,128]{3,2,1,0:T(2,128)S(1)}, f32[1,8,2,128]{3,2,1,0:T(2,128)S(1)}, u32[]{:S(2)}, u32[]{:S(2)}) collective-permute-start(f32[1,8,2,128]{3,2,1,0:T(2,128)S(1)} %get-tuple-element.229), channel_id=1, source_target_pairs={{0,2},{1,3},{4,6},{5,7},{8,10},{9,11},{12,14},{13,15},{16,18},{17,... | collective-permute-start | bytes 24584 | tf_op jit(solution)/shard_map/ppermute | solution.py:18
  117.0 8.6 %collective-permute-start.17 = (f32[1,8,2,128]{3,2,1,0:T(2,128)S(1)}, f32[1,8,2,128]{3,2,1,0:T(2,128)S(1)}, u32[]{:S(2)}, u32[]{:S(2)}) collective-permute-start(f32[1,8,2,128]{3,2,1,0:T(2,128)S(1)} %get-tuple-element.230), channel_id=1, source_target_pairs={{2,0},{3,1},{6,4},{7,5},{10,8},{11,9},{14,12},{15,13},{18,16},{19,... | collective-permute-start | bytes 24584 | tf_op jit(solution)/shard_map/ppermute | solution.py:21
  125.7 3.8 %collective-permute-start.18 = (f32[1,8,12,2]{3,2,1,0:T(8,128)S(1)}, f32[1,8,12,2]{3,2,1,0:T(8,128)S(1)}, u32[]{:S(2)}, u32[]{:S(2)}) collective-permute-start(f32[1,8,12,2]{3,2,1,0:T(8,128)S(1)} %get-tuple-element.217), channel_id=1, source_target_pairs={{0,1},{2,3},{4,5},{6,7},{8,9},{10,11},{12,13},{14,15},{16,17},{18,... | collective-permute-start | bytes 2312 | tf_op jit(solution)/shard_map/ppermute | solution.py:18
  127.0 3.1 %collective-permute-start.19 = (f32[1,8,12,2]{3,2,1,0:T(8,128)S(1)}, f32[1,8,12,2]{3,2,1,0:T(8,128)S(1)}, u32[]{:S(2)}, u32[]{:S(2)}) collective-permute-start(f32[1,8,12,2]{3,2,1,0:T(8,128)S(1)} %get-tuple-element.218), channel_id=1, source_target_pairs={{1,0},{3,2},{5,4},{7,6},{9,8},{11,10},{13,12},{15,14},{17,16},{19,... | collective-permute-start | bytes 2312 | tf_op jit(solution)/shard_map/ppermute | solution.py:21
  (24 other events, 174.6 us)
where the time goes:
time: 148 us; the launch traced here: 147 us
  starting transfers between devices  52.3 us (35%)
  waiting for transfers between devices  38.3 us (26%)
  matrix products  29.2 us (20%)
  local copies, waits for them, and re-layouts  19 us (13%)
  other arithmetic  5.93 us (4%)
  between operations  1.98 us (1%)
    dot_general x54, matrix products, convolve(): jnp.einsum('oc,czyx->ozyx', weight[:, :, tap], piece, precision=lax.Preci...  28.9 us
    ppermute x9, starting transfers between devices, with_halo(): lax.ppermute(lax.slice_in_dim(block, block.shape[dim] - width, None, axis...  23.4 us
    ppermute x6, waiting for transfers between devices, shifted(): lax.ppermute(value, axis, [(source, source + steps) for source in range(f...  20.7 us
    ppermute x9, waiting for transfers between devices, with_halo(): lax.ppermute(lax.slice_in_dim(block, 0, width, axis=dim), axis, backward)  17.6 us
    ppermute x6, starting transfers between devices, shifted(): lax.ppermute(value, axis, [(source, source + steps) for source in range(f...  17 us
    ppermute x9, starting transfers between devices, with_halo(): lax.ppermute(lax.slice_in_dim(block, 0, width, axis=dim), axis, backward)  11.9 us
    unnamed x76, local copies, waits for them, and re-layouts  10.2 us
    slice x4, local copies, waits for them, and re-layouts, convolve(): weight[:, :, tap]  5.59 us
  transfers between devices with their start and end apart: 24, of which 12 were waited for; matrix products, arithmetic and copies ran while one was open for 11% of the time, Pallas kernels for 0%

commit v1 on v0

v1 whole, which is shorter than its diff:
```python
import functools

import jax
import jax.numpy as jnp
from jax import lax
from jax.experimental import pallas as pl
from jax.experimental.pallas import tpu as pltpu
from jax.sharding import PartitionSpec as P

LANES = 128
F32 = jnp.float32
BF16 = jnp.bfloat16
MESH = pl.DeviceIdType.MESH


def split(value):
    high = value.astype(BF16)
    return high, (value - high.astype(F32)).astype(BF16)


def left_rows(weight):
    high, low = split(weight)
    return jnp.concatenate([high, high, low], axis=1)


def right_rows(high, low):
    return jnp.concatenate([high, low, high], axis=0)


def mxu(left, right):
    return jnp.dot(left, right, preferred_element_type=F32)


def lane_of(shape):
    return lax.broadcasted_iota(jnp.int32, shape, len(shape) - 1)


def row_of(shape):
    return lax.broadcasted_iota(jnp.int32, shape, 0)


def times(count, step, carry, backward=False):
    if count <= 16:
        for i in range(count):
            carry = step(count - 1 - i if backward else i, carry)
        return carry
    return lax.fori_loop(0, count, lambda i, c: step(count - 1 - i if backward else i, c), carry)


def aligned(start, unit):
    return start if isinstance(start, int) else pl.multiple_of(start, unit)


def gather_kernel(sizes, noisy_ref, m1, x1, where_ref, m1_send, m1_recv, x1_send, x1_recv):
    gz, gy, gx = sizes
    me = lax.axis_index("gz")
    at_y = lax.axis_index("gy")
    at_x = lax.axis_index("gx")
    low_slab = me == 0
    high_slab = me == gz - 1

    def exists(dy, dx):
        ok = None
        for where, step, count in ((at_y, dy, gy), (at_x, dx, gx)):
            if step == 0:
                continue
            here = where > 0 if step < 0 else where < count - 1
            ok = here if ok is None else ok & here
        return ok

    def when(ok, action):
        if ok is None:
            action()
        else:
            pl.when(ok)(action)

    def device(z, dy, dx):
        return {
            "win": lax.axis_index("win"),
            "gz": z,
            "gy": lax.rem(at_y + dy + gy, gy),
            "gx": lax.rem(at_x + dx + gx, gx),
        }

    def block(z):
        return z

    def peer(k):
        return lax.rem(me + k, gz)

    steps_y = (0,) + ((-1, 1) if gy > 1 else ())
    steps_x = (0,) + ((-1, 1) if gx > 1 else ())

    barrier = pltpu.get_barrier_semaphore()
    for dy in steps_y:
        for dx in steps_x:
            for k in range(gz):
                if (dy, dx, k) != (0, 0, 0):
                    def greet(dy=dy, dx=dx, k=k):
                        pl.semaphore_signal(
                            barrier, inc=1, device_id=device(peer(k), dy, dx), device_id_type=MESH
                        )
                    when(exists(dy, dx), greet)
    span_y = 1 + (at_y > 0).astype(jnp.int32) + (at_y < gy - 1).astype(jnp.int32)
    span_x = 1 + (at_x > 0).astype(jnp.int32) + (at_x < gx - 1).astype(jnp.int32)
    pl.semaphore_wait(barrier, gz * span_y * span_x - 1)

    def noisy_middle(dy, k):
        target = peer(k)
        return pltpu.make_async_remote_copy(
            src_ref=noisy_ref,
            dst_ref=m1.at[1 - dy, block(me)],
            send_sem=m1_send.at[dy + 1, k],
            recv_sem=m1_recv.at[1 - dy, me],
            device_id=device(target, dy, 0),
            device_id_type=MESH,
        )

    def noisy_edge(dy, dx):
        target = 0 if dx > 0 else gz - 1
        side = (dx + 1) // 2
        return pltpu.make_async_remote_copy(
            src_ref=noisy_ref,
            dst_ref=x1.at[1 - dy, block(me)],
            send_sem=x1_send.at[dy + 1, side],
            recv_sem=x1_recv.at[1 - dy, me],
            device_id=device(target, dy, dx),
            device_id_type=MESH,
        )

    sends = []
    for dy in steps_y:
        for k in range(gz - 1, -1, -1):
            if (dy, k) != (0, 0):
                sends.append((exists(dy, 0), functools.partial(noisy_middle, dy, k)))
    for dy in steps_y:
        for dx in steps_x:
            if dx != 0:
                sends.append((exists(dy, dx), functools.partial(noisy_edge, dy, dx)))
    for ok, make in sends:
        when(ok, lambda make=make: make().start())

    for i, value in enumerate((me, at_y, at_x)):
        where_ref[i] = value
    m1[1, block(me)] = noisy_ref[...]
    for index, ok in ((0, at_y == 0), (2, at_y == gy - 1)):
        def no_row(index=index):
            for z in range(gz):
                m1[index, z] = jnp.zeros(m1.shape[2:], F32)
                x1[index, z] = jnp.zeros(x1.shape[2:], F32)
        pl.when(ok)(no_row)
    no_edge = jnp.logical_not((low_slab & (at_x > 0)) | (high_slab & (at_x < gx - 1)))

    def no_neighbour():
        x1[...] = jnp.zeros(x1.shape, F32)

    pl.when(no_edge)(no_neighbour)
    for dy in steps_y:
        for k in range(gz):
            if (dy, k) != (0, 0):
                source = peer(k)
                def await_middle(dy=dy, source=source):
                    pltpu.make_async_remote_copy(
                        src_ref=noisy_ref,
                        dst_ref=m1.at[1 + dy, block(source)],
                        send_sem=m1_send.at[1 + dy, 0],
                        recv_sem=m1_recv.at[1 + dy, source],
                        device_id=device(source, dy, 0),
                        device_id_type=MESH,
                    ).wait_recv()
                when(exists(dy, 0), await_middle)
    for dy in steps_y:
        for dx in steps_x:
            if dx != 0:
                ok = exists(dy, dx) & (low_slab if dx < 0 else high_slab)
                for source in range(gz):
                    def await_edge(dy=dy, dx=dx, source=source):
                        pltpu.make_async_remote_copy(
                            src_ref=noisy_ref,
                            dst_ref=x1.at[1 + dy, block(source)],
                            send_sem=x1_send.at[1 + dy, 0],
                            recv_sem=x1_recv.at[1 + dy, source],
                            device_id=device(source, dy, dx),
                            device_id_type=MESH,
                        ).wait_recv()
                    pl.when(ok)(await_edge)

    for ok, make in sends:
        when(ok, lambda make=make: make().wait_send())


def layers_kernel(
    sizes, shape, where_ref, m1, x1, narrow_ref, wide_ref, bias_ref, packed, taps, taps_high, taps_low, product, fix
):
    gz, gy, gx = sizes
    bz, by, bx = shape
    depth = gz * bz
    slab = bx // gz
    out_lanes = by * slab
    tiles = taps.shape[0]
    me, at_y, at_x = where_ref[0], where_ref[1], where_ref[2]
    low_slab = me == 0
    high_slab = me == gz - 1
    taps[...] = jnp.zeros(taps.shape, F32)
    for plane in (0, depth + 1):
        product[plane] = jnp.zeros(product.shape[1:], F32)
    fix[...] = jnp.zeros(fix.shape, F32)
    first_left = left_rows(narrow_ref[0:96, :])
    second_left = left_rows(
        jnp.concatenate([wide_ref[48 * a : 48 * a + 32, :] for a in range(3)], axis=0)
    )
    first_bias = bias_ref[:, 0:1]
    second_bias = bias_ref[0:16, 1:2]
    head = bias_ref[0:16, 2:3]
    shape = (48, tiles * LANES)
    lane, row = lane_of(shape), row_of(shape)
    place_y = at_y * by + lane // slab - 1
    place_x = at_x * bx + me * slab + lane % slab + row // 16 - 1
    inside = (place_y >= 0) & (place_y < gy * by) & (place_x >= 0) & (place_x < gx * bx)
    mask = jnp.where(inside, 1.0, 0.0).astype(F32)

    lane = lane_of((depth, LANES))
    take_edge = (low_slab & (lane >= bx - 2)) | (high_slab & (lane < 2))
    windows = []
    turn = lax.rem(2 - me * slab + bx, bx)
    for line in range(by + 4):
        index, y = (0, by - 2 + line) if line < 2 else (1, line - 2) if line < by + 2 else (2, line - by - 2)
        rows = []
        for source in (m1, x1):
            rows.append(source[index, pl.ds(y, depth, stride=by), :])
        windows.append(pltpu.roll(jnp.where(take_edge, rows[1], rows[0]), turn, 1))
    wide_tiles = -(-(by + 4) * slab // LANES)
    for s in range(5):
        strips = []
        for tile in range(wide_tiles):
            strip = jnp.zeros((depth, LANES), F32)
            for line in range(by + 4):
                if line * slab // LANES == tile:
                    begin = line * slab % LANES
                    piece = pltpu.roll(windows[line], (begin - s) % LANES, 1)
                    strip = jnp.where((lane >= begin) & (lane < begin + slab), piece, strip)
            strips.append(strip)
        strips.append(jnp.zeros((depth, LANES), F32))
        for b in range(3):
            for tile in range(tiles):
                jump, off = divmod(b * slab, LANES)
                value = strips[min(tile + jump, wide_tiles)]
                if off:
                    after = strips[min(tile + jump + 1, wide_tiles)]
                    value = jnp.where(
                        lane < LANES - off,
                        pltpu.roll(value, LANES - off, 1),
                        pltpu.roll(after, LANES - off, 1),
                    )
                taps[tile, pl.ds(16 + b * 5 + s, depth, stride=16), :] = value
    high, low = split(taps[...])
    taps_high[...] = high
    taps_low[...] = low

    def forward(z, hidden):
        rows = pl.ds(aligned(z * 16, 16), 48)
        high = jnp.concatenate([taps_high[t, rows, :] for t in range(tiles)], axis=1)
        low = jnp.concatenate([taps_low[t, rows, :] for t in range(tiles)], axis=1)
        pre = mxu(first_left, right_rows(high, low))
        cand = jnp.tanh(pre[0:48])
        change = jax.nn.sigmoid(pre[48:96] + first_bias)
        hidden = hidden + change * (mask * cand - hidden)
        field = jnp.concatenate(
            [hidden[:, b * slab : b * slab + out_lanes] for b in range(3)], axis=0
        )
        high, low = split(field)
        product[z + 1] = mxu(second_left, right_rows(high, low))
        return hidden

    times(depth, forward, jnp.zeros((48, tiles * LANES), F32))

    def back(z, hidden):
        pre = product[z, 0:32] + product[z + 1, 32:64] + product[z + 2, 64:96]
        cand = jnp.tanh(pre[0:16])
        change = jax.nn.sigmoid(pre[16:32] + second_bias)
        hidden = hidden + change * (cand - hidden)
        fix[pl.ds(z + 2, 1), 0:out_lanes] = jnp.sum(head * hidden, axis=0, keepdims=True)
        return hidden

    times(depth, back, jnp.zeros((16, out_lanes), F32), True)
    for tile in range(-(-out_lanes // LANES)):
        lanes = slice(tile * LANES, (tile + 1) * LANES)
        centre = taps[tile, pl.ds(16 + 12, depth, stride=16), :]
        fix[2 : 2 + depth, lanes] = fix[2 : 2 + depth, lanes] + centre
    for target in range(gz):
        packed[target] = fix[bz * target : bz * target + bz + 4, :]


def scatter_kernel(sizes, packed, m3, x3, m3_send, m3_recv, x3_send, x3_recv):
    gz, gy, gx = sizes
    me = lax.axis_index("gz")
    at_y = lax.axis_index("gy")
    at_x = lax.axis_index("gx")
    low_slab = me == 0
    high_slab = me == gz - 1

    def exists(dy, dx):
        ok = None
        for where, step, count in ((at_y, dy, gy), (at_x, dx, gx)):
            if step == 0:
                continue
            here = where > 0 if step < 0 else where < count - 1
            ok = here if ok is None else ok & here
        return ok

    def when(ok, action):
        if ok is None:
            action()
        else:
            pl.when(ok)(action)

    def device(z, dy, dx):
        return {
            "win": lax.axis_index("win"),
            "gz": z,
            "gy": lax.rem(at_y + dy + gy, gy),
            "gx": lax.rem(at_x + dx + gx, gx),
        }

    def peer(k):
        return lax.rem(me + k, gz)

    steps_y = (0,) + ((-1, 1) if gy > 1 else ())
    steps_x = (0,) + ((-1, 1) if gx > 1 else ())

    barrier = pltpu.get_barrier_semaphore()
    for dy in steps_y:
        for dx in steps_x:
            for k in range(gz):
                if (dy, dx, k) != (0, 0, 0):
                    def greet(dy=dy, dx=dx, k=k):
                        pl.semaphore_signal(
                            barrier, inc=1, device_id=device(peer(k), dy, dx), device_id_type=MESH
                        )
                    when(exists(dy, dx), greet)
    span_y = 1 + (at_y > 0).astype(jnp.int32) + (at_y < gy - 1).astype(jnp.int32)
    span_x = 1 + (at_x > 0).astype(jnp.int32) + (at_x < gx - 1).astype(jnp.int32)
    pl.semaphore_wait(barrier, gz * span_y * span_x - 1)

    def clean_middle(dy, k):
        target = peer(k)
        return pltpu.make_async_remote_copy(
            src_ref=packed.at[target],
            dst_ref=m3.at[1 - dy, me],
            send_sem=m3_send.at[dy + 1, k],
            recv_sem=m3_recv.at[1 - dy, me],
            device_id=device(target, dy, 0),
            device_id_type=MESH,
        )

    def clean_edge(dy, dx, k):
        target = peer(k)
        side = (dx + 1) // 2
        return pltpu.make_async_remote_copy(
            src_ref=packed.at[target],
            dst_ref=x3.at[1 - dy, 1 - side],
            send_sem=x3_send.at[dy + 1, side, k],
            recv_sem=x3_recv.at[1 - dy, 1 - side],
            device_id=device(target, dy, dx),
            device_id_type=MESH,
        )

    late = []
    for dy in steps_y:
        for k in range(gz - 1, -1, -1):
            if (dy, k) != (0, 0):
                late.append((exists(dy, 0), functools.partial(clean_middle, dy, k)))
    for dy in steps_y:
        for dx in steps_x:
            if dx != 0:
                ok = exists(dy, dx) & (high_slab if dx > 0 else low_slab)
                for k in range(gz):
                    late.append((ok, functools.partial(clean_edge, dy, dx, k)))
    for ok, make in late:
        when(ok, lambda make=make: make().start())
    m3[1, me] = packed[me]
    for index, ok in ((0, at_y == 0), (2, at_y == gy - 1)):
        def no_row_again(index=index):
            m3[index] = jnp.zeros(m3.shape[1:], F32)
            x3[index] = jnp.zeros(x3.shape[1:], F32)
        pl.when(ok)(no_row_again)
    for side, ok in ((0, at_x == 0), (1, at_x == gx - 1)):
        def no_side(side=side):
            for index in range(3):
                x3[index, side] = jnp.zeros(x3.shape[2:], F32)
        pl.when(ok)(no_side)
    for dy in steps_y:
        for k in range(gz):
            if (dy, k) != (0, 0):
                source = peer(k)
                def await_clean(dy=dy, source=source):
                    pltpu.make_async_remote_copy(
                        src_ref=packed.at[0],
                        dst_ref=m3.at[1 + dy, source],
                        send_sem=m3_send.at[1 + dy, 0],
                        recv_sem=m3_recv.at[1 + dy, source],
                        device_id=device(source, dy, 0),
                        device_id_type=MESH,
                    ).wait_recv()
                when(exists(dy, 0), await_clean)
    for dy in steps_y:
        for dx in steps_x:
            if dx != 0:
                side = (dx + 1) // 2
                source = gz - 1 if dx < 0 else 0
                def await_side(dy=dy, dx=dx, side=side, source=source):
                    pltpu.make_async_remote_copy(
                        src_ref=packed.at[0],
                        dst_ref=x3.at[1 + dy, side],
                        send_sem=x3_send.at[1 + dy, side, 0],
                        recv_sem=x3_recv.at[1 + dy, side],
                        device_id=device(source, dy, dx),
                        device_id_type=MESH,
                    ).wait_recv()
                when(exists(dy, dx), await_side)

    for ok, make in late:
        when(ok, lambda make=make: make().wait_send())


def segment_kernel(
    sizes,
    where_ref,
    m3,
    x3,
    narrow_ref,
    wide_ref,
    bias_ref,
    clean_ref,
    out_ref,
    middle_ref,
    edge_ref,
    taps,
    result,
):
    gz, gy, gx = sizes
    lines, planes, bx = middle_ref.shape
    by, bz = lines - 4, planes - 4
    me, at_y, at_x = where_ref[0], where_ref[1], where_ref[2]
    slab = bx // gz
    lane = lane_of((bz + 4, LANES))
    for line in range(by + 4):
        index, y = (0, by - 2 + line) if line < 2 else (1, line - 2) if line < by + 2 else (2, line - by - 2)
        tile, off = divmod(y * slab, LANES)
        lanes = slice(tile * LANES, (tile + 1) * LANES)
        whole = jnp.zeros((bz + 4, LANES), F32)
        for source in range(gz):
            begin = source * slab
            piece = pltpu.roll(m3[index, source, :, lanes], (begin - off) % LANES, 1)
            whole = jnp.where((lane >= begin) & (lane < begin + slab), piece, whole)
        middle_ref[line] = whole
        before = pltpu.roll(x3[index, 0, :, lanes], (bx - off - slab) % LANES, 1)
        after = pltpu.roll(x3[index, 1, :, lanes], (-off) % LANES, 1)
        edge_ref[line] = jnp.where(lane < LANES // 2, after, before)

    in_left = left_rows(narrow_ref[96:144, :])
    out_left = left_rows(
        jnp.concatenate([wide_ref[48 * a + 32 : 48 * a + 48, :] for a in range(3)], axis=0)
    )
    in_bias = bias_ref[:, 3:4]
    out_bias = bias_ref[0:16, 4:5]
    for y in range(by + 2):
        taps[y, pl.ds(15, planes, stride=16), :] = jnp.zeros((planes, bx), F32)
    lane = lane_of((planes, bx))
    for line in range(lines):
        middle, edge = middle_ref[line], edge_ref[line]
        for s in range(5):
            value = middle
            if s < 2:
                value = pltpu.roll(jnp.where(lane >= bx - (2 - s), edge, middle), 2 - s, 1)
            if s > 2:
                value = pltpu.roll(jnp.where(lane < s - 2, edge, middle), bx - (s - 2), 1)
            for b in range(3):
                if 0 <= line - b < by + 2:
                    taps[line - b, pl.ds(b * 5 + s, planes, stride=16), :] = value

    for z in range(bz):
        clean_ref[z] = middle_ref[2 : 2 + by, 2 + z, :]
    shape = (48, (by + 2) * bx)
    lane, row = lane_of(shape), row_of(shape)
    place_y = at_y * by + lane // bx - 1
    place_x = at_x * bx + lane % bx + row // 16 - 1
    inside = (place_y >= 0) & (place_y < gy * by) & (place_x >= 0) & (place_x < gx * bx)
    mask = jnp.where(inside, 1.0, 0.0).astype(F32)
    partial = []
    for z in range(bz + 2):
        rows = jnp.concatenate([taps[y, z * 16 : z * 16 + 48, :] for y in range(by + 2)], axis=1)
        high, low = split(rows)
        grown = jnp.maximum(mxu(in_left, right_rows(high, low)) + in_bias, 0.0) * mask
        if z == 0:
            grown = grown * jnp.where(me > 0, 1.0, 0.0).astype(F32)
        if z == bz + 1:
            grown = grown * jnp.where(me < gz - 1, 1.0, 0.0).astype(F32)
        high, low = split(grown)
        field_high = jnp.concatenate([high[:, b * bx : (b + by) * bx] for b in range(3)], axis=0)
        field_low = jnp.concatenate([low[:, b * bx : (b + by) * bx] for b in range(3)], axis=0)
        partial.append(mxu(out_left, right_rows(field_high, field_low)))
        if z >= 2:
            total = partial[z - 2][0:16] + partial[z - 1][16:32] + partial[z][32:48] + out_bias
            for y in range(by):
                result[pl.ds((z - 2) * by + y, 16, stride=bz * by), :] = total[:, y * bx : (y + 1) * bx]
    out_ref[...] = result[0 : 16 * bz * by, :]


def narrow_rows(weight):
    parts = weight.shape[0] // 16
    kernel = weight.reshape(parts, 16, 3, 3, 3)
    moved = jnp.stack(
        [jnp.pad(kernel, ((0, 0),) * 4 + ((c, 2 - c),)) for c in range(3)], axis=1
    ).reshape(parts * 48, 3, 15)
    return jnp.pad(moved, ((0, 0), (0, 0), (0, 1))).reshape(parts * 48, 48)


def wide_rows(weight):
    outs, ins = weight.shape[0], weight.shape[1]
    return weight.reshape(outs, ins, 3, 9).transpose(2, 0, 3, 1).reshape(3 * outs, 9 * ins)


def body(sizes, noisy, first_weight, first_bias, second_weight, second_bias, head_weight,
         seg_weight_in, seg_bias_in, seg_weight_out, seg_bias_out):
    gz, gy, gx = sizes
    bz, by, bx = noisy.shape
    depth = gz * bz
    slab = bx // gz
    tiles = -(-(by + 2) * slab // LANES)
    out_lanes = by * slab
    out_tiles = -(-out_lanes // LANES)
    narrow = narrow_rows(jnp.concatenate([first_weight, seg_weight_in], axis=0))
    wide = wide_rows(jnp.concatenate([second_weight, seg_weight_out], axis=0))
    biases = jnp.stack([first_bias, second_bias, head_weight, seg_bias_in, seg_bias_out], axis=1)
    biases = jnp.tile(biases, (3, 1))
    vmem = pl.BlockSpec(memory_space=pltpu.VMEM)
    dma = pltpu.SemaphoreType.DMA
    smem = pl.BlockSpec(memory_space=pltpu.SMEM)
    blocks = jax.ShapeDtypeStruct((3, gz, bz * by, bx), F32)
    m1, x1, where = pl.pallas_call(
        functools.partial(gather_kernel, sizes),
        out_shape=[blocks, blocks, jax.ShapeDtypeStruct((3,), jnp.int32)],
        in_specs=[vmem],
        out_specs=[vmem, vmem, smem],
        scratch_shapes=[dma((3, gz)), dma((3, gz)), dma((3, 2)), dma((3, gz))],
        compiler_params=pltpu.CompilerParams(collective_id=0, has_side_effects=True),
        name="gather",
    )(noisy.reshape(bz * by, bx))
    packed = pl.pallas_call(
        functools.partial(layers_kernel, sizes, (bz, by, bx)),
        out_shape=jax.ShapeDtypeStruct((gz, bz + 4, out_tiles * LANES), F32),
        in_specs=[smem] + [vmem] * 5,
        out_specs=vmem,
        scratch_shapes=[
            pltpu.VMEM((tiles, (depth + 2) * 16, LANES), F32),
            pltpu.VMEM((tiles, (depth + 2) * 16, LANES), BF16),
            pltpu.VMEM((tiles, (depth + 2) * 16, LANES), BF16),
            pltpu.VMEM((depth + 2, 96, out_lanes), F32),
            pltpu.VMEM((depth + 16, out_tiles * LANES), F32),
        ],
        name="layers",
    )(where, m1.reshape(3, depth * by, bx), x1.reshape(3, depth * by, bx), narrow, wide, biases)
    m3, x3 = pl.pallas_call(
        functools.partial(scatter_kernel, sizes),
        out_shape=[
            jax.ShapeDtypeStruct((3, gz, bz + 4, out_tiles * LANES), F32),
            jax.ShapeDtypeStruct((3, 2, bz + 4, out_tiles * LANES), F32),
        ],
        in_specs=[vmem],
        out_specs=[vmem] * 2,
        scratch_shapes=[dma((3, gz)), dma((3, gz)), dma((3, 2, gz)), dma((3, 2))],
        compiler_params=pltpu.CompilerParams(collective_id=1, has_side_effects=True),
        name="scatter",
    )(packed)
    clean, features = pl.pallas_call(
        functools.partial(segment_kernel, sizes),
        out_shape=[
            jax.ShapeDtypeStruct((bz, by, bx), F32),
            jax.ShapeDtypeStruct((16 * bz * by, bx), F32),
        ],
        in_specs=[smem] + [vmem] * 5,
        out_specs=[vmem] * 2,
        scratch_shapes=[
            pltpu.VMEM((by + 4, bz + 4, bx), F32),
            pltpu.VMEM((by + 4, bz + 4, bx), F32),
            pltpu.VMEM((by + 2, (bz + 5) * 16, bx), F32),
            pltpu.VMEM((17 * bz * by, bx), F32),
        ],
        name="segment",
    )(where, m3, x3, narrow, wide, biases)
    return clean, features.reshape(16, bz, by, bx)


def solution(mesh):
    sizes = (mesh.shape["gz"], mesh.shape["gy"], mesh.shape["gx"])
    in_specs = (P(("win", "gz"), "gy", "gx"), P(), P(), P(), P(), P(), P(), P(), P(), P())
    out_specs = (P(("win", "gz"), "gy", "gx"), P(None, ("win", "gz"), "gy", "gx"))
    return jax.shard_map(
        functools.partial(body, sizes), mesh=mesh, in_specs=in_specs, out_specs=out_specs, check_vma=False
    )
```

time: 148 us -> 36.5 us (0.25)
  starting transfers between devices: 52.3 us -> 0 us
  waiting for transfers between devices: 38.3 us -> 0 us
  Pallas kernels: 0 us -> 29.4 us
  matrix products: 29.2 us -> 0 us
  local copies, waits for them, and re-layouts: 19 us -> 4.75 us
  other arithmetic: 5.93 us -> 1.19 us
    ppermute x24 -> x0, starting transfers between devices: 52.3 us -> none  [the longest x9 23.4 us: with_halo(): lax.ppermute(lax.slice_in_dim(block, block.shape[dim] - width, None, axis...]
    ppermute x24 -> x0, waiting for transfers between devices: 38.3 us -> none  [the longest x6 20.7 us: shifted(): lax.ppermute(value, axis, [(source, source + steps) for source in range(f...]
    pallas_call x0 -> x4, Pallas kernels: none -> 29.4 us  [the longest x1 12.6 us: body(): pl.pallas_call(functools.partial(gather_kernel, sizes), out_shape=[blocks...]
    dot_general x55 -> x0, matrix products: 29.2 us -> none  [the longest x54 28.9 us: convolve(): jnp.einsum('oc,czyx->ozyx', weight[:, :, tap], piece, precision=lax.Preci...]
    unnamed x76 -> x6, local copies, waits for them, and re-layouts: 10.2 us -> 1.01 us
    slice x11 -> x0, local copies, waits for them, and re-layouts: 6.69 us -> none  [the longest x4 5.59 us: convolve(): weight[:, :, tap]]
    mul x7 -> x0, other arithmetic: 3.5 us -> none  [the longest x1 2.97 us: body(): grown * (mask_z[:, None, None] * mask_y[None, :, None] * mask_x[None, Non...]
    reshape x1 -> x6, local copies, waits for them, and re-layouts: 0.01 us -> 2.03 us  [the longest x3 1.05 us: wide_rows(): weight.reshape(outs, ins, 3, 9).transpose(2, 0, 3, 1)]
  transfers between devices with their start and end apart: 24 -> 0, of which waited for: 12 -> 0; matrix products, arithmetic and copies ran while one was open for 11% -> 0% of each run, Pallas kernels for 0% -> 0%
where the time goes in v1:
time: 36.5 us; the launch traced here: 36.1 us
  Pallas kernels  29.4 us (81%)
  local copies, waits for them, and re-layouts  4.75 us (13%)
  other arithmetic  1.19 us (3%)
  between operations  0.74 us (2%)
    pallas_call x1, Pallas kernels, body(): pl.pallas_call(functools.partial(gather_kernel, sizes), out_shape=[blocks...  12.6 us
    pallas_call x1, Pallas kernels, body(): pl.pallas_call(functools.partial(scatter_kernel, sizes), out_shape=[jax.S...  8.72 us
    pallas_call x1, Pallas kernels, body(): pl.pallas_call(functools.partial(layers_kernel, sizes, (bz, by, bx)), out...  4.19 us
    pallas_call x1, Pallas kernels, body(): pl.pallas_call(functools.partial(segment_kernel, sizes), out_shape=[jax.S...  3.96 us
    reshape x3, local copies, waits for them, and re-layouts, wide_rows(): weight.reshape(outs, ins, 3, 9).transpose(2, 0, 3, 1)  1.05 us
    unnamed x6, local copies, waits for them, and re-layouts  1.01 us
    another operation x2, local copies, waits for them, and re-layouts, body(): jnp.stack([first_bias, second_bias, head_weight, seg_bias_in, seg_bias_ou...  0.86 us
    concatenate x1, other arithmetic, body(): narrow = narrow_rows(jnp.concatenate([first_weight, seg_weight_in], axis=0))  0.83 us

profile of v1, /device:TPU:0, one launch (start us, length us, event | category | flops | bytes accessed | tf_op | source)
XLA Modules:
  0.0 36.1 jit_solution(12101183427657900624)
XLA Ops:
  0.6 0.0 copy-start.1
  0.6 0.8 %stack.39 = f32[16,5]{0,1:T(8,128)S(1)} concatenate(f32[16,1]{0,1:T(1,128)} %bitcast.35, f32[16,1]{0,1:T(1,128)} %bitcast.36, f32[16,1]{0,1:T(1,128)} %bitcast.37, f32[16,1]{0,1:T(1,128)} %bitcast.38, f32[16,1]{0,1:T(1,128)} %bitcast.39), dimensions={1} | concatenate | bytes 640 | tf_op jit(solution)/shard_map/stack | solution.py:535
  1.4 0.1 copy.22
  1.5 0.8 %copy.17 = f32[16,1,27]{0,1,2:T(1,128)S(1)} copy(f32[16,1,27]{2,1,0:T(1,128)} %param.16) | data formatting | bytes 3456 | tf_op args[6]
  2.3 0.8 %maximum_reduce_fusion = f32[48,27]{0,1:T(8,128)S(1)} fusion(f32[16,1,27]{0,1,2:T(1,128)S(1)} %copy.17, f32[32,1,27]{0,1,2:T(1,128)} %param.11), kind=kLoop, calls=%fused_computation.5 | loop fusion | flops 1296 | bytes 10368 | tf_op jit(solution)/shard_map/concatenate | solution.py:533
  3.1 0.0 copy-start
  3.1 0.6 %tile.4 = f32[3,16,5]{2,1,0:T(8,128)} broadcast(f32[16,5]{1,0:T(8,128)S(1)} %copy.22), dimensions={1,2} | broadcast | bytes 1280 | tf_op jit(solution)/shard_map/tile | solution.py:536
  3.7 0.1 reshape.38
  3.8 0.0 copy-done.1
  3.8 0.2 copy.20
  4.0 0.0 copy-done
  4.1 0.1 pad_maximum_fusion.1
  4.2 0.1 copy.28
  4.3 0.2 reshape.42
  4.5 0.8 %copy.24.wide_ref = f32[144,144]{1,0:T(8,128)} copy(f32[144,144]{0,1:T(8,128)S(1)} %reshape.42) | data formatting | bytes 165888 | tf_op jit(solution)/shard_map/reshape | solution.py:521
  5.3 0.1 copy.18
  5.4 0.1 copy.19
  5.5 0.2 pad_maximum_fusion
  5.8 0.2 reshape.39
  5.9 0.7 %copy.23.narrow_ref = f32[144,48]{1,0:T(8,128)} copy(f32[144,48]{0,1:T(8,128)S(1)} %bitcast.31) | data formatting | bytes 55296 | tf_op jit(solution)/shard_map/reshape | solution.py:516
  6.7 12.6 %gather.1 = (f32[3,4,32,128]{3,2,1,0:T(8,128)}, f32[3,4,32,128]{3,2,1,0:T(8,128)}, s32[3]{0:T(128)}) custom-call(f32[32,128]{1,0:T(8,128)} %bitcast.34), custom_call_target="tpu_custom_call" | custom-call | tf_op jit(solution)/shard_map/gather/pallas_call | solution.py:541
  19.2 4.2 %layers.1.packed = f32[4,8,256]{2,1,0:T(8,128)} custom-call(s32[3]{0:T(128)} %get-tuple-element.9.where_ref, f32[3,128,128]{2,1,0:T(8,128)} %bitcast.32, f32[3,128,128]{2,1,0:T(8,128)} %bitcast.33, f32[144,48]{1,0:T(8,128)} %copy.23.narrow_ref, f32[144,144]{1,0:T(8,128)} %copy.24.wide_ref, f32[48,5]{1,0:T(8,128)} %bitcast.29), custom_call_target="tpu_custom_call" | custom-call | tf_op jit(solution)/shard_map/layers/pallas_call | solution.py:550
  23.4 8.7 %scatter.1 = (f32[3,4,8,256]{3,2,1,0:T(8,128)}, f32[3,2,8,256]{3,2,1,0:T(8,128)}) custom-call(f32[4,8,256]{2,1,0:T(8,128)} %layers.1.packed), custom_call_target="tpu_custom_call" | custom-call | tf_op jit(solution)/shard_map/scatter/pallas_call | solution.py:564
  32.2 4.0 %segment.1 = (f32[4,8,128]{2,1,0:T(8,128)}, f32[512,128]{1,0:T(8,128)}) custom-call(s32[3]{0:T(128)} %get-tuple-element.9.where_ref, f32[3,4,8,256]{3,2,1,0:T(8,128)} %get-tuple-element.12.m3, f32[3,2,8,256]{3,2,1,0:T(8,128)} %get-tuple-element.13.x3, f32[144,48]{1,0:T(8,128)} %copy.23.narrow_ref, f32[144,144]{1,0:T(8,128)} %copy.24.wide_ref, f32[48,5]{1,0:T(8,128)} %bitcast.30), custom_call_target="tpu_custom_call" | custom-call | tf_op jit(solution)/shard_map/segment/pallas_call | solution.py:576
  (3 shorter events, 0.1 us)
Async XLA Ops:
  0.6 3.2 %copy-start.1 = (f32[16,16,27]{2,1,0:T(8,128)S(1)}, f32[16,16,27]{2,1,0:T(8,128)}, u32[]{:S(2)}) copy-start(f32[16,16,27]{2,1,0:T(8,128)} %param.18) | copy-start | bytes 82948
  3.1 0.9 %copy-start = (f32[32,16,27]{0,1,2:T(8,128)S(1)}, f32[32,16,27]{0,1,2:T(8,128)}, u32[]{:S(2)}) copy-start(f32[32,16,27]{0,1,2:T(8,128)} %param.13) | copy-start | bytes 165892

commit v2 on v1

--- a/solution.py
+++ b/solution.py
@@ -39,6 +39,13 @@
     return lax.broadcasted_iota(jnp.int32, shape, 0)
 
 
+def column(row_ref):
+    count = row_ref.shape[1]
+    shape = (count, count)
+    spread = jnp.broadcast_to(row_ref[...], shape)
+    return jnp.sum(jnp.where(row_of(shape) == lane_of(shape), spread, 0.0), axis=1, keepdims=True)
+
+
 def times(count, step, carry, backward=False):
     if count <= 16:
         for i in range(count):
@@ -51,7 +58,7 @@
     return start if isinstance(start, int) else pl.multiple_of(start, unit)
 
 
-def gather_kernel(sizes, noisy_ref, m1, x1, where_ref, m1_send, m1_recv, x1_send, x1_recv):
+def gather_kernel(sizes, by, noisy_ref, m1, x1, my, xy, where_ref, halo, m1_send, m1_recv, x1_send, x1_recv):
     gz, gy, gx = sizes
     me = lax.axis_index("gz")
     at_y = lax.axis_index("gy")
@@ -82,14 +89,23 @@
             "gx": lax.rem(at_x + dx + gx, gx),
         }
 
-    def block(z):
-        return z
-
     def peer(k):
         return lax.rem(me + k, gz)
 
     steps_y = (0,) + ((-1, 1) if gy > 1 else ())
     steps_x = (0,) + ((-1, 1) if gx > 1 else ())
+
+    for side, first in ((0, 0), (1, by - 2)):
+        for z in range(noisy_ref.shape[0] // by):
+            halo[side, 2 * z : 2 * z + 2, :] = noisy_ref[z * by + first : z * by + first + 2, :]
+
+    def payload(dy):
+        return noisy_ref if dy == 0 else halo.at[(dy + 1) // 2]
+
+    def slot(edge, dy, z):
+        if dy == 0:
+            return (x1 if edge else m1).at[z]
+        return (xy if edge else my).at[(dy + 1) // 2, z]
 
     barrier = pltpu.get_barrier_semaphore()
     for dy in steps_y:
@@ -108,8 +124,8 @@
     def noisy_middle(dy, k):
         target = peer(k)
         return pltpu.make_async_remote_copy(
-            src_ref=noisy_ref,
-            dst_ref=m1.at[1 - dy, block(me)],
+            src_ref=payload(dy),
+            dst_ref=slot(False, -dy, me),
             send_sem=m1_send.at[dy + 1, k],
             recv_sem=m1_recv.at[1 - dy, me],
             device_id=device(target, dy, 0),
@@ -120,8 +136,8 @@
         target = 0 if dx > 0 else gz - 1
         side = (dx + 1) // 2
         return pltpu.make_async_remote_copy(
-            src_ref=noisy_ref,
-            dst_ref=x1.at[1 - dy, block(me)],
+            src_ref=payload(dy),
+            dst_ref=slot(True, -dy, me),
             send_sem=x1_send.at[dy + 1, side],
             recv_sem=x1_recv.at[1 - dy, me],
             device_id=device(target, dy, dx),
@@ -142,17 +158,18 @@
 
     for i, value in enumerate((me, at_y, at_x)):
         where_ref[i] = value
-    m1[1, block(me)] = noisy_ref[...]
-    for index, ok in ((0, at_y == 0), (2, at_y == gy - 1)):
+    m1[me] = noisy_ref[...]
+    for index, ok in ((0, at_y == 0), (1, at_y == gy - 1)):
         def no_row(index=index):
             for z in range(gz):
-                m1[index, z] = jnp.zeros(m1.shape[2:], F32)
-                x1[index, z] = jnp.zeros(x1.shape[2:], F32)
+                my[index, z] = jnp.zeros(my.shape[2:], F32)
+                xy[index, z] = jnp.zeros(xy.shape[2:], F32)
         pl.when(ok)(no_row)
     no_edge = jnp.logical_not((low_slab & (at_x > 0)) | (high_slab & (at_x < gx - 1)))
 
     def no_neighbour():
         x1[...] = jnp.zeros(x1.shape, F32)
+        xy[...] = jnp.zeros(xy.shape, F32)
 
     pl.when(no_edge)(no_neighbour)
     for dy in steps_y:
@@ -161,8 +178,8 @@
                 source = peer(k)
                 def await_middle(dy=dy, source=source):
                     pltpu.make_async_remote_copy(
-                        src_ref=noisy_ref,
-                        dst_ref=m1.at[1 + dy, block(source)],
+                        src_ref=payload(dy),
+                        dst_ref=slot(False, dy, source),
                         send_sem=m1_send.at[1 + dy, 0],
                         recv_sem=m1_recv.at[1 + dy, source],
                         device_id=device(source, dy, 0),
@@ -176,8 +193,8 @@
                 for source in range(gz):
                     def await_edge(dy=dy, dx=dx, source=source):
                         pltpu.make_async_remote_copy(
-                            src_ref=noisy_ref,
-                            dst_ref=x1.at[1 + dy, block(source)],
+                            src_ref=payload(dy),
+                            dst_ref=slot(True, dy, source),
                             send_sem=x1_send.at[1 + dy, 0],
                             recv_sem=x1_recv.at[1 + dy, source],
                             device_id=device(source, dy, dx),
@@ -190,7 +207,7 @@
 
 
 def layers_kernel(
-    sizes, shape, where_ref, m1, x1, narrow_ref, wide_ref, bias_ref, packed, taps, taps_high, taps_low, product, fix
+    sizes, shape, where_ref, m1, x1, my, xy, narrow_ref, wide_ref, first_ref, second_ref, head_ref, packed, taps, taps_high, taps_low, product, fix
 ):
     gz, gy, gx = sizes
     bz, by, bx = shape
@@ -209,9 +226,9 @@
     second_left = left_rows(
         jnp.concatenate([wide_ref[48 * a : 48 * a + 32, :] for a in range(3)], axis=0)
     )
-    first_bias = bias_ref[:, 0:1]
-    second_bias = bias_ref[0:16, 1:2]
-    head = bias_ref[0:16, 2:3]
+    first_bias = jnp.concatenate([column(first_ref)] * 3, axis=0)
+    second_bias = column(second_ref)
+    head = column(head_ref)
     shape = (48, tiles * LANES)
     lane, row = lane_of(shape), row_of(shape)
     place_y = at_y * by + lane // slab - 1
@@ -224,10 +241,13 @@
     windows = []
     turn = lax.rem(2 - me * slab + bx, bx)
     for line in range(by + 4):
-        index, y = (0, by - 2 + line) if line < 2 else (1, line - 2) if line < by + 2 else (2, line - by - 2)
         rows = []
-        for source in (m1, x1):
-            rows.append(source[index, pl.ds(y, depth, stride=by), :])
+        for source, beside in ((m1, my), (x1, xy)):
+            if 2 <= line < by + 2:
+                rows.append(source[pl.ds(line - 2, depth, stride=by), :])
+            else:
+                side, place = (0, line) if line < 2 else (1, line - by - 2)
+                rows.append(beside[side, pl.ds(place, depth, stride=2), :])
         windows.append(pltpu.roll(jnp.where(take_edge, rows[1], rows[0]), turn, 1))
     wide_tiles = -(-(by + 4) * slab // LANES)
     for s in range(5):
@@ -291,7 +311,7 @@
         packed[target] = fix[bz * target : bz * target + bz + 4, :]
 
 
-def scatter_kernel(sizes, packed, m3, x3, m3_send, m3_recv, x3_send, x3_recv):
+def scatter_kernel(sizes, by, slab, packed, m3, x3, m3_send, m3_recv, x3_send, x3_recv):
     gz, gy, gx = sizes
     me = lax.axis_index("gz")
     at_y = lax.axis_index("gy")
@@ -342,11 +362,17 @@
     span_x = 1 + (at_x > 0).astype(jnp.int32) + (at_x < gx - 1).astype(jnp.int32)
     pl.semaphore_wait(barrier, gz * span_y * span_x - 1)
 
+    lanes = packed.shape[2]
+    last = (by - 2) * slab // LANES * LANES
+
+    def part(dy):
+        return {0: slice(0, lanes), 1: slice(last, last + LANES), -1: slice(0, LANES)}[dy]
+
     def clean_middle(dy, k):
         target = peer(k)
         return pltpu.make_async_remote_copy(
-            src_ref=packed.at[target],
-            dst_ref=m3.at[1 - dy, me],
+            src_ref=packed.at[target, :, part(dy)],
+            dst_ref=m3.at[1 - dy, me, :, part(dy)],
             send_sem=m3_send.at[dy + 1, k],
             recv_sem=m3_recv.at[1 - dy, me],
             device_id=device(target, dy, 0),
@@ -357,8 +383,8 @@
         target = peer(k)
         side = (dx + 1) // 2
         return pltpu.make_async_remote_copy(
-            src_ref=packed.at[target],
-            dst_ref=x3.at[1 - dy, 1 - side],
+            src_ref=packed.at[target, :, part(dy)],
+            dst_ref=x3.at[1 - dy, 1 - side, :, part(dy)],
             send_sem=x3_send.at[dy + 1, side, k],
             recv_sem=x3_recv.at[1 - dy, 1 - side],
             device_id=device(target, dy, dx),
@@ -395,8 +421,8 @@
                 source = peer(k)
                 def await_clean(dy=dy, source=source):
                     pltpu.make_async_remote_copy(
-                        src_ref=packed.at[0],
-                        dst_ref=m3.at[1 + dy, source],
+                        src_ref=packed.at[0, :, part(-dy)],
+                        dst_ref=m3.at[1 + dy, source, :, part(-dy)],
                         send_sem=m3_send.at[1 + dy, 0],
                         recv_sem=m3_recv.at[1 + dy, source],
                         device_id=device(source, dy, 0),
@@ -410,8 +436,8 @@
                 source = gz - 1 if dx < 0 else 0
                 def await_side(dy=dy, dx=dx, side=side, source=source):
                     pltpu.make_async_remote_copy(
-                        src_ref=packed.at[0],
-                        dst_ref=x3.at[1 + dy, side],
+                        src_ref=packed.at[0, :, part(-dy)],
+                        dst_ref=x3.at[1 + dy, side, :, part(-dy)],
                         send_sem=x3_send.at[1 + dy, side, 0],
                         recv_sem=x3_recv.at[1 + dy, side],
                         device_id=device(source, dy, dx),
@@ -430,7 +456,8 @@
     x3,
     narrow_ref,
     wide_ref,
-    bias_ref,
+    in_ref,
+    last_ref,
     clean_ref,
     out_ref,
     middle_ref,
@@ -462,8 +489,8 @@
     out_left = left_rows(
         jnp.concatenate([wide_ref[48 * a + 32 : 48 * a + 48, :] for a in range(3)], axis=0)
     )
-    in_bias = bias_ref[:, 3:4]
-    out_bias = bias_ref[0:16, 4:5]
+    in_bias = jnp.concatenate([column(in_ref)] * 3, axis=0)
+    out_bias = column(last_ref)
     for y in range(by + 2):
         taps[y, pl.ds(15, planes, stride=16), :] = jnp.zeros((planes, bx), F32)
     lane = lane_of((planes, bx))
@@ -532,25 +559,27 @@
     out_tiles = -(-out_lanes // LANES)
     narrow = narrow_rows(jnp.concatenate([first_weight, seg_weight_in], axis=0))
     wide = wide_rows(jnp.concatenate([second_weight, seg_weight_out], axis=0))
-    biases = jnp.stack([first_bias, second_bias, head_weight, seg_bias_in, seg_bias_out], axis=1)
-    biases = jnp.tile(biases, (3, 1))
+    rows = [v.reshape(1, -1) for v in (first_bias, second_bias, head_weight, seg_bias_in, seg_bias_out)]
     vmem = pl.BlockSpec(memory_space=pltpu.VMEM)
     dma = pltpu.SemaphoreType.DMA
     smem = pl.BlockSpec(memory_space=pltpu.SMEM)
-    blocks = jax.ShapeDtypeStruct((3, gz, bz * by, bx), F32)
-    m1, x1, where = pl.pallas_call(
-        functools.partial(gather_kernel, sizes),
-        out_shape=[blocks, blocks, jax.ShapeDtypeStruct((3,), jnp.int32)],
+    blocks = jax.ShapeDtypeStruct((gz, bz * by, bx), F32)
+    halos = jax.ShapeDtypeStruct((2, gz, bz * 2, bx), F32)
+    m1, x1, my, xy, where = pl.pallas_call(
+        functools.partial(gather_kernel, sizes, by),
+        out_shape=[blocks, blocks, halos, halos, jax.ShapeDtypeStruct((3,), jnp.int32)],
         in_specs=[vmem],
-        out_specs=[vmem, vmem, smem],
-        scratch_shapes=[dma((3, gz)), dma((3, gz)), dma((3, 2)), dma((3, gz))],
+        out_specs=[vmem] * 4 + [smem],
+        scratch_shapes=[
+            pltpu.VMEM((2, bz * 2, bx), F32), dma((3, gz)), dma((3, gz)), dma((3, 2)), dma((3, gz))
+        ],
         compiler_params=pltpu.CompilerParams(collective_id=0, has_side_effects=True),
         name="gather",
     )(noisy.reshape(bz * by, bx))
     packed = pl.pallas_call(
         functools.partial(layers_kernel, sizes, (bz, by, bx)),
         out_shape=jax.ShapeDtypeStruct((gz, bz + 4, out_tiles * LANES), F32),
-        in_specs=[smem] + [vmem] * 5,
+        in_specs=[smem] + [vmem] * 9,
         out_specs=vmem,
         scratch_shapes=[
             pltpu.VMEM((tiles, (depth + 2) * 16, LANES), F32),
@@ -560,9 +589,18 @@
             pltpu.VMEM((depth + 16, out_tiles * LANES), F32),
         ],
         name="layers",
-    )(where, m1.reshape(3, depth * by, bx), x1.reshape(3, depth * by, bx), narrow, wide, biases)
+    )(
+        where,
+        m1.reshape(depth * by, bx),
+        x1.reshape(depth * by, bx),
+        my.reshape(2, depth * 2, bx),
+        xy.reshape(2, depth * 2, bx),
+        narrow,
+        wide,
+        *rows[:3],
+    )
     m3, x3 = pl.pallas_call(
-        functools.partial(scatter_kernel, sizes),
+        functools.partial(scatter_kernel, sizes, by, slab),
         out_shape=[
             jax.ShapeDtypeStruct((3, gz, bz + 4, out_tiles * LANES), F32),
             jax.ShapeDtypeStruct((3, 2, bz + 4, out_tiles * LANES), F32),
@@ -579,7 +617,7 @@
             jax.ShapeDtypeStruct((bz, by, bx), F32),
             jax.ShapeDtypeStruct((16 * bz * by, bx), F32),
         ],
-        in_specs=[smem] + [vmem] * 5,
+        in_specs=[smem] + [vmem] * 6,
         out_specs=[vmem] * 2,
         scratch_shapes=[
             pltpu.VMEM((by + 4, bz + 4, bx), F32),
@@ -588,7 +626,7 @@
             pltpu.VMEM((17 * bz * by, bx), F32),
         ],
         name="segment",
-    )(where, m3, x3, narrow, wide, biases)
+    )(where, m3, x3, narrow, wide, *rows[3:])
     return clean, features.reshape(16, bz, by, bx)
 
 

time: 36.5 us -> 32.9 us (0.901)
  local copies, waits for them, and re-layouts: 4.75 us -> 3.24 us
  Pallas kernels: 29.4 us -> 28.1 us
  other arithmetic: 1.19 us -> 0.49 us
    another operation x3 -> x0, local copies, waits for them, and re-layouts: 1.47 us -> none  [the longest x2 0.86 us: body(): jnp.stack([first_bias, second_bias, head_weight, seg_bias_in, seg_bias_ou...]
    pallas_call x2, Pallas kernels: 21.3 us -> 20 us  [the longest x1 11.3 us: body(): pl.pallas_call(functools.partial(gather_kernel, sizes, by), out_shape=[bl...]
    concatenate x1, other arithmetic: 0.83 us -> 0.11 us  [body(): narrow = narrow_rows(jnp.concatenate([first_weight, seg_weight_in], axis=0))]
    unnamed x6 -> x8, local copies, waits for them, and re-layouts: 1.01 us -> 0.99 us
where the time goes in v2:
time: 32.9 us; the launch traced here: 32.6 us
  Pallas kernels  28.1 us (85%)
  local copies, waits for them, and re-layouts  3.24 us (10%)
  between operations  0.75 us (2%)
  other arithmetic  0.49 us (1%)
    pallas_call x1, Pallas kernels, body(): pl.pallas_call(functools.partial(gather_kernel, sizes, by), out_shape=[bl...  11.3 us
    pallas_call x1, Pallas kernels, body(): pl.pallas_call(functools.partial(scatter_kernel, sizes, by, slab), out_sh...  8.62 us
    pallas_call x1, Pallas kernels, body(): pl.pallas_call(functools.partial(layers_kernel, sizes, (bz, by, bx)), out...  4.12 us
    pallas_call x1, Pallas kernels, body(): pl.pallas_call(functools.partial(segment_kernel, sizes), out_shape=[jax.S...  4.03 us
    reshape x3, local copies, waits for them, and re-layouts, wide_rows(): weight.reshape(outs, ins, 3, 9).transpose(2, 0, 3, 1)  1.03 us
    unnamed x8, local copies, waits for them, and re-layouts  0.99 us
    reshape x1, local copies, waits for them, and re-layouts, narrow_rows(): return jnp.pad(moved, ((0, 0), (0, 0), (0, 1))).reshape(parts * 48, 48)  0.73 us

profile of v2, /device:TPU:0, one launch (start us, length us, event | category | flops | bytes accessed | tf_op | source)
XLA Modules:
  0.0 32.6 jit_solution(4151272656552947549)
XLA Ops:
  0.6 0.0 copy-start.2
  0.6 0.8 %copy.16 = f32[16,1,27]{0,1,2:T(1,128)S(1)} copy(f32[16,1,27]{2,1,0:T(1,128)} %param.16) | data formatting | bytes 3456 | tf_op args[6]
  1.4 0.0 copy-done.2
  1.4 0.1 maximum_reduce_fusion
  1.6 0.1 reshape.57
  1.7 0.1 copy.17
  1.8 0.1 copy.18
  1.9 0.2 pad_maximum_fusion
  2.2 0.2 reshape.58
  2.3 0.0 copy-start.1
  2.3 0.7 %copy.21.narrow_ref = f32[144,48]{1,0:T(8,128)} copy(f32[144,48]{0,1:T(8,128)S(1)} %bitcast.30) | data formatting | bytes 55296 | tf_op jit(solution)/shard_map/reshape | solution.py:543
  3.1 0.0 copy-start
  3.1 11.3 %gather.1 = (f32[4,32,128]{2,1,0:T(8,128)}, f32[4,32,128]{2,1,0:T(8,128)}, f32[2,4,8,128]{3,2,1,0:T(8,128)}, f32[2,4,8,128]{3,2,1,0:T(8,128)}, s32[3]{0:T(128)}) custom-call(f32[32,128]{1,0:T(8,128)} %bitcast.35), custom_call_target="tpu_custom_call" | custom-call | tf_op jit(solution)/shard_map/gather/pallas_call | solution.py:568
  14.4 0.0 copy-done.1
  14.4 0.2 copy.19
  14.6 0.0 copy-done
  14.6 0.1 pad_maximum_fusion.1
  14.8 0.1 copy.26
  14.9 0.2 reshape.61
  15.1 0.8 %copy.22.wide_ref = f32[144,144]{1,0:T(8,128)} copy(f32[144,144]{0,1:T(8,128)S(1)} %reshape.61) | data formatting | bytes 165888 | tf_op jit(solution)/shard_map/reshape | solution.py:548
  15.8 4.1 %layers.1.packed = f32[4,8,256]{2,1,0:T(8,128)} custom-call(s32[3]{0:T(128)} %get-tuple-element.11.where_ref, f32[128,128]{1,0:T(8,128)} %bitcast.31, f32[128,128]{1,0:T(8,128)} %bitcast.32, f32[2,32,128]{2,1,0:T(8,128)} %bitcast.33, f32[2,32,128]{2,1,0:T(8,128)} %bitcast.34, f32[144,48]{1,0:T(8,128)} %copy.21.narrow_ref, f32[144,144]{1,0:T(8,128)} %copy.22.wide_ref, ...), custom_call_target="tpu_custom_call" | custom-call | tf_op jit(solution)/shard_map/layers/pallas_call | solution.py:579
  19.9 8.6 %scatter.1 = (f32[3,4,8,256]{3,2,1,0:T(8,128)}, f32[3,2,8,256]{3,2,1,0:T(8,128)}) custom-call(f32[4,8,256]{2,1,0:T(8,128)} %layers.1.packed), custom_call_target="tpu_custom_call" | custom-call | tf_op jit(solution)/shard_map/scatter/pallas_call | solution.py:602
  28.6 4.0 %segment.1 = (f32[4,8,128]{2,1,0:T(8,128)}, f32[512,128]{1,0:T(8,128)}) custom-call(s32[3]{0:T(128)} %get-tuple-element.11.where_ref, f32[3,4,8,256]{3,2,1,0:T(8,128)} %get-tuple-element.16.m3, f32[3,2,8,256]{3,2,1,0:T(8,128)} %get-tuple-element.17.x3, f32[144,48]{1,0:T(8,128)} %copy.21.narrow_ref, f32[144,144]{1,0:T(8,128)} %copy.22.wide_ref, ...), custom_call_target="tpu_custom_call" | custom-call | tf_op jit(solution)/shard_map/segment/pallas_call | solution.py:614
  (3 shorter events, 0.1 us)
Async XLA Ops:
  0.6 0.8 %copy-start.2 = (f32[32,1,27]{0,1,2:T(1,128)S(1)}, f32[32,1,27]{0,1,2:T(1,128)}, u32[]{:S(2)}) copy-start(f32[32,1,27]{0,1,2:T(1,128)} %param.11) | copy-start | bytes 10372
  2.3 12.1 %copy-start.1 = (f32[16,16,27]{2,1,0:T(8,128)S(1)}, f32[16,16,27]{2,1,0:T(8,128)}, u32[]{:S(2)}) copy-start(f32[16,16,27]{2,1,0:T(8,128)} %param.18) | copy-start | bytes 82948
  3.1 11.6 %copy-start = (f32[32,16,27]{0,1,2:T(8,128)S(1)}, f32[32,16,27]{0,1,2:T(8,128)}, u32[]{:S(2)}) copy-start(f32[32,16,27]{0,1,2:T(8,128)} %param.13) | copy-start | bytes 165892
